TPU v7x, 32 devices: a whole 2x2x4 slice. The times are simulated.
32 devices in a mesh: parts: 2 (over y), seq: 8 (over z, core), rep: 2 (over x), head: 1.
Axes of the slice: x: 2, y: 2, z: 4, core: 2. Of those that a mesh axis runs over, the one named last changes fastest.
Arguments:
- activations: bfloat16 [4, 1024, 2048], P(('parts', 'rep'), 'seq', 'head'), parts along dimension 0, may hold values from -6 to 6
- value_weight: bfloat16 [2048, 2048], P(('seq', 'rep'), 'head'), may hold values from -0.125 to 0.125
- query_in: bfloat16 [4, 1024, 2048], P(('parts', 'rep'), 'seq', 'head'), parts along dimension 0, may hold values from -6 to 6
- key_in: bfloat16 [4, 1024, 2048], P(('parts', 'rep'), 'seq', 'head'), parts along dimension 0, may hold values from -6 to 6
- grad_out: bfloat16 [4, 1024, 2048], P(('parts', 'rep'), 'seq', 'head'), parts along dimension 0, may hold values from -6 to 6
- conv_kernel: float32 [3, 4, 2048], P(None, None, 'head'), may hold values from -3 to 3
- log_gate: float32 [4, 16, 1024], P(('parts', 'rep'), 'head', 'seq'), parts along dimension 0, as said below
Outputs:
- attn_out: bfloat16 [4, 1024, 2048], P(('parts', 'rep'), 'seq', 'head'), parts along dimension 0
- grad_query: bfloat16 [4, 1024, 2048], P(('parts', 'rep'), 'seq', 'head'), parts along dimension 0
- grad_key: bfloat16 [4, 1024, 2048], P(('parts', 'rep'), 'seq', 'head'), parts along dimension 0
- grad_x: bfloat16 [4, 1024, 2048], P(('parts', 'rep'), 'seq', 'head'), parts along dimension 0
- grad_w: float32 [4096, 2048], P(('parts', 'seq', 'rep'), 'head'), parts along dimension 0
- grad_conv: float32 [6, 4, 2048], P('parts', None, 'head'), parts along dimension 0
There are 2 independent parts, one for each index of `parts`. A program takes and returns all parts, laid end to end along the dimension named above; an argument that names none is the same for every part. Nothing has to cross between parts.
Inputs may be any that keep to these rules, and one draw needn't show every extreme that they name: `log_gate`: every entry is below zero.
All inputs are finite; a program needn't handle non-finite values.
Results may differ from a plain program's by a relative error of at most 0.015.
Values may be sent and summed in bfloat16 or wider, within the bound.
A program may use at most 128 MiB of HBM per device.

v0:
```python
import math
import jax
import jax.numpy as jnp
from jax import lax
from jax.sharding import PartitionSpec as P

EPSILON = 1e-06


def shifted(block, axis, distance):
    devices = range(lax.axis_size(axis))
    route = [(i - distance, i) for i in devices if i - distance in devices]
    return lax.ppermute(block, axis, route)


def prefix(part, axis, combine, identity, reverse):
    count = lax.axis_size(axis)
    place = lax.axis_index(axis)
    ahead = count - 1 - place if reverse else place
    gathered = jax.tree.map(lambda a: lax.all_gather(a, axis), part)
    state = jax.tree.map(lambda a, e: jnp.zeros_like(a) + jnp.asarray(e, a.dtype), part, identity)

    def one(step, state):
        source = count - 1 - step if reverse else step
        return combine(
            state, jax.tree.map(lambda a: lax.dynamic_index_in_dim(a, source, 0, False), gathered)
        )

    return lax.fori_loop(0, ahead, one, state)


def carried_in(value, axis, combine, identity, reverse):
    length, mine = (lax.axis_size(axis), lax.axis_index(axis))
    everything = jax.tree.map(
        lambda part, kind: lax.all_gather(part.astype(kind), axis),
        value,
        (jnp.bfloat16, jnp.bfloat16),
    )
    start = jax.tree.map(
        lambda part, zero: jnp.broadcast_to(jnp.asarray(zero, part.dtype), part.shape),
        value,
        identity,
    )

    def step(k, before):
        at = length - 1 - k if reverse else k
        reached = at > mine if reverse else at < mine
        new = combine(
            before, jax.tree.map(lambda part, own: part[at].astype(own.dtype), everything, value)
        )
        return jax.tree.map(lambda a, b: jnp.where(reached, a, b), new, before)

    return lax.fori_loop(0, length, step, start)


def scanned(decay, state, axis, reverse):
    count = lax.axis_size(axis)
    direction = -1 if reverse else 1
    distance = 1
    while distance < count:
        far_decay, far_state = shifted((decay, state), axis, direction * distance)
        decay, state = chain_join((far_decay, far_state), (decay, state))
        distance *= 2
    return shifted(state, axis, direction)


def chain_join(earlier, following):
    return (earlier[0] * following[0], following[0][:, None, None] * earlier[1] + following[1])


def causal_filter(stream_rows, previous, kernel_taps):
    rim_rows = previous.shape[0]
    length = stream_rows.shape[0]
    extended = jnp.concatenate([previous, stream_rows], axis=0).astype(jnp.float32)
    result = jnp.zeros(stream_rows.shape, jnp.float32)
    for offset in range(kernel_taps.shape[0]):
        result = (
            result + kernel_taps[offset] * extended[rim_rows - offset : rim_rows - offset + length]
        )
    return result


def filter_back(post_rows, following_rows, kernel_taps):
    length = post_rows.shape[0]
    extended = jnp.concatenate([post_rows, following_rows], axis=0)
    result = jnp.zeros(post_rows.shape, jnp.float32)
    for offset in range(kernel_taps.shape[0]):
        result = result + kernel_taps[offset] * extended[offset : offset + length]
    return result


def tap_sums(post_rows, stream_rows, previous, kernel_width):
    rim_rows = previous.shape[0]
    length = stream_rows.shape[0]
    extended = jnp.concatenate([previous, stream_rows], axis=0).astype(jnp.float32)
    return jnp.stack(
        [
            jnp.sum(post_rows * extended[rim_rows - offset : rim_rows - offset + length], axis=0)
            for offset in range(kernel_width)
        ]
    )


def local(activations, value_weight, query_in, key_in, grad_out, conv_kernel, log_gate):
    tok_rows = query_in.shape[1]
    channels = query_in.shape[2]
    head_count = log_gate.shape[1]
    head_size = channels // head_count
    kernel_width = conv_kernel.shape[1]
    rim_rows = kernel_width - 1
    grad_scale = 1.0 / math.sqrt(lax.axis_size("seq") * lax.axis_size("rep") * tok_rows)
    query_rows = query_in[0]
    key_rows = key_in[0]
    gathered = lax.all_gather(activations, "head", axis=2, tiled=True)[0]
    columns = gathered
    value_f32 = jnp.dot(
        columns,
        lax.all_gather(value_weight, ("seq", "rep"), axis=0, tiled=True),
        preferred_element_type=jnp.float32,
    )
    value_raw = value_f32.astype(jnp.bfloat16)
    before_all = shifted(
        jnp.stack(
            [
                query_rows[tok_rows - rim_rows :],
                key_rows[tok_rows - rim_rows :],
                value_raw[tok_rows - rim_rows :],
            ]
        ),
        "seq",
        1,
    )
    before = (before_all[0], before_all[1], before_all[2])
    raw_rows = (query_rows, key_rows, value_raw)
    convolved = [
        causal_filter(raw_rows[which], before[which], conv_kernel[which]).astype(jnp.bfloat16)
        for which in range(3)
    ]
    query_heads = convolved[0].reshape(tok_rows, head_count, head_size)
    key_heads = convolved[1].reshape(tok_rows, head_count, head_size)
    value_heads = convolved[2].reshape(tok_rows, head_count, head_size)
    cumulative = jnp.cumsum(log_gate[0], axis=1)
    final_cum = cumulative[:, -1]
    block_decay = jnp.exp(final_cum)
    rising = jnp.exp(cumulative).T[:, :, None]
    shrink = jnp.exp(final_cum[:, None] - cumulative).T[:, :, None]
    mixing = jnp.exp(-jnp.abs(cumulative[:, :, None] - cumulative[:, None, :]))
    scores = (
        mixing
        * jnp.einsum("thd,shd->hts", query_heads, key_heads, preferred_element_type=jnp.float32)
    ).astype(jnp.bfloat16)
    fwd_sum = jnp.einsum(
        "thd,the->hde",
        (shrink * key_heads).astype(jnp.bfloat16),
        value_heads,
        preferred_element_type=jnp.float32,
    )
    back_sum = jnp.einsum(
        "thd,the->hde",
        (rising * key_heads).astype(jnp.bfloat16),
        value_heads,
        preferred_element_type=jnp.float32,
    )
    identity = (
        jnp.ones((head_count,), jnp.float32),
        jnp.zeros((head_count, head_size, head_size), jnp.float32),
    )
    left_b = scanned(block_decay, fwd_sum, "seq", False).astype(jnp.bfloat16)
    right_b = scanned(block_decay, back_sum, "seq", True).astype(jnp.bfloat16)
    attn = rising * jnp.einsum(
        "thd,hde->the", query_heads, left_b, preferred_element_type=jnp.float32
    )
    attn = attn + shrink * jnp.einsum(
        "thd,hde->the", query_heads, right_b, preferred_element_type=jnp.float32
    )
    attn = attn + jnp.einsum(
        "hts,she->the", scores, value_heads, preferred_element_type=jnp.float32
    )
    root_mean = jnp.sqrt(jnp.mean(attn * attn, axis=2, keepdims=True) + EPSILON)
    normed = attn / root_mean
    attn_out = normed.astype(jnp.bfloat16).reshape(1, tok_rows, channels)
    upstream = grad_out[0].reshape(tok_rows, head_count, head_size).astype(jnp.float32)
    grad_attn = (
        (upstream - normed * jnp.mean(upstream * normed, axis=2, keepdims=True)) / root_mean
    ).astype(jnp.bfloat16)
    grad_scores = (
        mixing
        * jnp.einsum("the,she->hts", grad_attn, value_heads, preferred_element_type=jnp.float32)
    ).astype(jnp.bfloat16)
    fwd_grad = jnp.einsum(
        "thd,the->hde",
        (shrink * query_heads).astype(jnp.bfloat16),
        grad_attn,
        preferred_element_type=jnp.float32,
    )
    back_grad = jnp.einsum(
        "thd,the->hde",
        (rising * query_heads).astype(jnp.bfloat16),
        grad_attn,
        preferred_element_type=jnp.float32,
    )
    left_gb = scanned(block_decay, fwd_grad, "seq", False).astype(jnp.bfloat16)
    right_gb = scanned(block_decay, back_grad, "seq", True).astype(jnp.bfloat16)
    query_post = rising * jnp.einsum(
        "the,hde->thd", grad_attn, left_b, preferred_element_type=jnp.float32
    )
    query_post = query_post + shrink * jnp.einsum(
        "the,hde->thd", grad_attn, right_b, preferred_element_type=jnp.float32
    )
    query_post = query_post + jnp.einsum(
        "hts,shd->thd", grad_scores, key_heads, preferred_element_type=jnp.float32
    )
    key_post = rising * jnp.einsum(
        "the,hde->thd", value_heads, left_gb, preferred_element_type=jnp.float32
    )
    key_post = key_post + shrink * jnp.einsum(
        "the,hde->thd", value_heads, right_gb, preferred_element_type=jnp.float32
    )
    key_post = key_post + jnp.einsum(
        "hts,thd->shd", grad_scores, query_heads, preferred_element_type=jnp.float32
    )
    value_post = rising * jnp.einsum(
        "thd,hde->the", key_heads, left_gb, preferred_element_type=jnp.float32
    )
    value_post = value_post + shrink * jnp.einsum(
        "thd,hde->the", key_heads, right_gb, preferred_element_type=jnp.float32
    )
    value_post = value_post + jnp.einsum(
        "hts,the->she", scores, grad_attn, preferred_element_type=jnp.float32
    )
    post_grads = jnp.stack(
        [
            query_post.reshape(tok_rows, channels),
            key_post.reshape(tok_rows, channels),
            value_post.reshape(tok_rows, channels),
        ]
    )
    following = shifted(post_grads[:, :rim_rows].astype(jnp.bfloat16), "seq", -1).astype(
        jnp.float32
    )
    grad_query = filter_back(post_grads[0], following[0], conv_kernel[0]).astype(jnp.bfloat16)
    grad_key = filter_back(post_grads[1], following[1], conv_kernel[1]).astype(jnp.bfloat16)
    grad_value = filter_back(post_grads[2], following[2], conv_kernel[2]).astype(jnp.bfloat16)
    kernel_terms = (
        jnp.stack(
            [
                tap_sums(post_grads[which], raw_rows[which], before[which], kernel_width)
                for which in range(3)
            ]
        )
        * grad_scale
    )
    grad_conv = lax.psum(kernel_terms, ("seq", "rep"))
    partial_x = lax.dot_general(
        grad_value,
        lax.all_gather(value_weight, ("seq", "rep"), axis=0, tiled=True),
        (((1,), (1,)), ((), ())),
        preferred_element_type=jnp.float32,
    )
    grad_x = lax.psum_scatter(
        partial_x[None].astype(jnp.bfloat16), "head", scatter_dimension=2, tiled=True
    )
    feature_rows = lax.all_to_all(gathered, ("seq", "rep"), 1, 0, tiled=True)
    grad_value_all = lax.all_gather(grad_value, ("seq", "rep"), axis=0, tiled=True)
    grad_w = (
        lax.dot_general(
            feature_rows,
            grad_value_all,
            (((0,), (0,)), ((), ())),
            preferred_element_type=jnp.float32,
        )
        * grad_scale
    )
    return (attn_out, grad_query[None], grad_key[None], grad_x, grad_w, grad_conv)


def solution(mesh):
    placed = (
        P(("parts", "rep"), "seq", "head"),
        P(("seq", "rep"), "head"),
        P(("parts", "rep"), "seq", "head"),
        P(("parts", "rep"), "seq", "head"),
        P(("parts", "rep"), "seq", "head"),
        P(None, None, "head"),
        P(("parts", "rep"), "head", "seq"),
    )
    return jax.shard_map(
        local,
        mesh=mesh,
        in_specs=placed,
        out_specs=(
            P(("parts", "rep"), "seq", "head"),
            P(("parts", "rep"), "seq", "head"),
            P(("parts", "rep"), "seq", "head"),
            P(("parts", "rep"), "seq", "head"),
            P(("parts", "seq", "rep"), "head"),
            P("parts", None, "head"),
        ),
        check_vma=False,
    )
```

profile of v0, /device:TPU:0, one launch (start us, length us, event | category | flops | bytes accessed | tf_op | source)
XLA Modules:
  0.0 546.2 jit_solution(14763116871213756074)
XLA Ops:
  11.9 75.3 %all-gather.3.cloned.1.call-done = bf16[2048,2048]{1,0:T(8,128)(2,1)} async-done(((bf16[128,2048]{1,0:T(8,128)(2,1)}), bf16[2048,2048]{1,0:T(8,128)(2,1)}) %all-gather.3.cloned.1.call-update) | async-done | bytes 8388624 | tf_op jit(solution)/shard_map/all_gather | solution.py:118
  87.2 4.6 convolution_convert_fusion.1
  92.0 2.2 collective-permute-start.2
  99.4 3.4 collective-permute-start.3
  105.0 4.4 collective-permute-done.9
  111.2 14.4 %collective-permute-start.4 = (f32[16,128,128]{2,1,0:T(8,128)S(1)}, f32[16,128,128]{2,1,0:T(8,128)S(1)}, u32[]{:S(2)}, u32[]{:S(2)}) collective-permute-start(f32[16,128,128]{2,1,0:T(8,128)S(1)} %get-tuple-element.65), channel_id=1, source_target_pairs={{0,4},{2,6},{4,8},{6,10},{8,12},{10,14},{1,5},{3,7},{5,9},{7,11},{... | collective-permute-start | bytes 3145736 | tf_op jit(solution)/shard_map/ppermute | solution.py:13
  125.6 3.6 collective-permute-start
  130.6 1.7 collective-permute-done.7
  132.3 14.0 %collective-permute-done.10 = f32[16,128,128]{2,1,0:T(8,128)S(1)} collective-permute-done((f32[16,128,128]{2,1,0:T(8,128)S(1)}, f32[16,128,128]{2,1,0:T(8,128)S(1)}, u32[]{:S(2)}, u32[]{:S(2)}) %collective-permute-start.10) | collective-permute-done | bytes 1048608 | tf_op jit(solution)/shard_map/ppermute | solution.py:13
  150.0 10.6 %collective-permute-start.5 = (f32[16,128,128]{2,1,0:T(8,128)}, f32[16,128,128]{2,1,0:T(8,128)}, u32[]{:S(2)}, u32[]{:S(2)}) collective-permute-start(f32[16,128,128]{2,1,0:T(8,128)} %multiply_add_fusion.10), channel_id=1, source_target_pairs={{0,8},{2,10},{4,12},{6,14},{1,9},{3,11},{5,13},{7,15},{16,24},{18,... | collective-permute-start | bytes 3145736 | tf_op jit(solution)/shard_map/ppermute | solution.py:13
  160.6 2.2 copy.108
  162.8 4.0 collective-permute-start.1
  168.1 13.9 %collective-permute-done.1 = f32[16]{0:T(128)S(1)} collective-permute-done((f32[16]{0:T(128)S(1)}, f32[16]{0:T(128)S(1)}, u32[]{:S(2)}, u32[]{:S(2)}) %collective-permute-start.1) | collective-permute-done | bytes 96 | tf_op jit(solution)/shard_map/ppermute | solution.py:13
  183.3 2.0 copy.99
  185.3 1.7 fusion.18
  187.1 14.1 %collective-permute-done.11 = f32[16,128,128]{2,1,0:T(8,128)} collective-permute-done((f32[16,128,128]{2,1,0:T(8,128)}, f32[16,128,128]{2,1,0:T(8,128)}, u32[]{:S(2)}, u32[]{:S(2)}) %collective-permute-start.11) | collective-permute-done | bytes 1048608 | tf_op jit(solution)/shard_map/ppermute | solution.py:13
  201.2 1.7 multiply_add_fusion.6
  204.3 1.7 multiply_add_fusion.9
  206.1 3.2 collective-permute-start.6
  213.6 16.0 %collective-permute-start.13 = (f32[16,128,128]{2,1,0:T(8,128)S(1)}, f32[16,128,128]{2,1,0:T(8,128)S(1)}, u32[]{:S(2)}, u32[]{:S(2)}) collective-permute-start(f32[16,128,128]{2,1,0:T(8,128)S(1)} %fusion.53), channel_id=1, source_target_pairs={{0,2},{2,4},{4,6},{6,8},{8,10},{10,12},{12,14},{1,3},{3,5},{5,7},{... | collective-permute-start | bytes 3145736 | tf_op jit(solution)/shard_map/ppermute | solution.py:13
  231.8 4.3 collective-permute-done.17
  238.0 14.6 %collective-permute-start.14 = (f32[16,128,128]{2,1,0:T(8,128)S(1)}, f32[16,128,128]{2,1,0:T(8,128)S(1)}, u32[]{:S(2)}, u32[]{:S(2)}) collective-permute-start(f32[16,128,128]{2,1,0:T(8,128)S(1)} %get-tuple-element.61), channel_id=1, source_target_pairs={{0,4},{2,6},{4,8},{6,10},{8,12},{10,14},{1,5},{3,7},{5,9},{7,11},{... | collective-permute-start | bytes 3145736 | tf_op jit(solution)/shard_map/ppermute | solution.py:13
  253.4 19.0 %collective-permute-done.18 = f32[16,128,128]{2,1,0:T(8,128)S(1)} collective-permute-done((f32[16,128,128]{2,1,0:T(8,128)S(1)}, f32[16,128,128]{2,1,0:T(8,128)S(1)}, u32[]{:S(2)}, u32[]{:S(2)}) %collective-permute-start.18) | collective-permute-done | bytes 1048608 | tf_op jit(solution)/shard_map/ppermute | solution.py:13
  276.2 9.0 %collective-permute-start.15 = (f32[16,128,128]{2,1,0:T(8,128)}, f32[16,128,128]{2,1,0:T(8,128)}, u32[]{:S(2)}, u32[]{:S(2)}) collective-permute-start(f32[16,128,128]{2,1,0:T(8,128)} %multiply_add_fusion.4), channel_id=1, source_target_pairs={{0,8},{2,10},{4,12},{6,14},{1,9},{3,11},{5,13},{7,15},{16,24},{18,... | collective-permute-start | bytes 3145736 | tf_op jit(solution)/shard_map/ppermute | solution.py:13
  287.2 2.0 copy.156
  290.8 36.1 %collective-permute-done.19 = f32[16,128,128]{2,1,0:T(8,128)} collective-permute-done((f32[16,128,128]{2,1,0:T(8,128)}, f32[16,128,128]{2,1,0:T(8,128)}, u32[]{:S(2)}, u32[]{:S(2)}) %collective-permute-start.19) | collective-permute-done | bytes 1048608 | tf_op jit(solution)/shard_map/ppermute | solution.py:13
  326.9 1.7 multiply_add_fusion
  330.1 1.7 multiply_add_fusion.3
  331.8 3.2 collective-permute-start.16
  336.9 1.7 fusion.90
  338.6 2.0 copy.157
  340.6 1.7 fusion.2
  342.5 1.5 fusion.89
  344.0 2.0 copy.158
  348.1 2.6 copy.159
  350.7 4.3 collective-permute-done.21
  355.0 4.4 multiply_reduce_fusion.3
  359.5 2.0 copy.129
  361.5 29.8 %all_to_all.19 = bf16[128,16,128]{0,2,1:T(8,128)(2,1)} all-to-all(bf16[128,16,128]{0,2,1:T(8,128)(2,1)} %bitcast.200), channel_id=1, replica_groups=mesh['parts'=2,'seq'=8,'rep'=2,'head'=1] {'seq','rep'}, dimensions={1} | all-to-all | bytes 1048576 | tf_op jit(solution)/shard_map/all_to_all | solution.py:263
  391.3 2.0 copy.130
  394.7 2.1 copy.139
  398.2 4.1 multiply_reduce_fusion.11
  402.4 1.7 multiply_reduce_fusion.7
  404.9 8.2 %fusion.1 = bf16[1,128,2048]{2,1,0:T(8,128)(2,1)} fusion(bf16[128,2048]{1,0:T(8,128)(2,1)S(1)} %copy-done.10, bf16[2048,2048]{1,0:T(8,128)(2,1)} %all-gather.3.cloned.1.call-done), kind=kOutput, calls=%fused_computation.4 | convolution fusion | flops 1074003968 | bytes 9437184 | tf_op jit(solution)/shard_map/dot_general | solution.py:254
  413.1 33.6 %all-gather.5.cloned.1.call-done = bf16[2048,2048]{1,0:T(8,128)(2,1)} async-done(((bf16[128,2048]{1,0:T(8,128)(2,1)}), bf16[2048,2048]{1,0:T(8,128)(2,1)}) %all-gather.5.cloned.1.call-update) | async-done | bytes 8388624 | tf_op jit(solution)/shard_map/all_gather | solution.py:264
  446.7 5.8 %fusion = f32[128,2048]{0,1:T(8,128)S(1)} fusion(bf16[2048,2048]{1,0:T(8,128)(2,1)} %all-gather.5.cloned.1.call-done, bf16[2048,128]{1,0:T(8,128)(2,1)S(1)} %bitcast.204), kind=kOutput, calls=%fused_computation.1 | convolution fusion | flops 1074003968 | bytes 9961472 | tf_op jit(solution)/shard_map/dot_general | solution.py:266
  453.8 84.3 %all-reduce.2.cloned.1.call-done = f32[3,4,2048]{2,1,0:T(4,128)} async-done(((f32[3,4,2048]{2,1,0:T(4,128)}), f32[3,4,2048]{2,1,0:T(4,128)}) %all-reduce.2.cloned.1.call-update) | async-done | bytes 98320 | tf_op jit(solution)/shard_map/psum | solution.py:253
  538.1 1.5 copy.188
  (135 shorter events, 49.7 us)
Async XLA Ops:
  7.2 80.1 %copy-start.15 = (bf16[1,128,2048]{2,1,0:T(8,128)(2,1)S(1)}, bf16[1,128,2048]{2,1,0:T(8,128)(2,1)}, u32[]{:S(2)}) copy-start(bf16[1,128,2048]{2,1,0:T(8,128)(2,1)} %param.7) | copy-start | bytes 1572868
  7.2 80.1 %all-gather.3.cloned.1.call-start = ((), (), s32[]{:S(2)}) async-start(), calls=%async_computation.1 | async-start | bytes 8912896 | tf_op jit(solution)/shard_map/all_gather | solution.py:118
  7.9 438.8 %all-gather.5.cloned.1.call-start = ((), (), s32[]{:S(2)}) async-start(), calls=%async_computation.2 | async-start | bytes 8912896 | tf_op jit(solution)/shard_map/all_gather | solution.py:264
  11.9 83.2 %copy-start.23 = (bf16[1,128,2048]{2,1,0:T(8,128)(2,1)S(1)}, bf16[1,128,2048]{2,1,0:T(8,128)(2,1)}, u32[]{:S(2)}) copy-start(bf16[1,128,2048]{2,1,0:T(8,128)(2,1)} %param.10) | copy-start | bytes 1572868
  11.9 83.2 %copy-start.24 = (bf16[1,128,2048]{2,1,0:T(8,128)(2,1)S(1)}, bf16[1,128,2048]{2,1,0:T(8,128)(2,1)}, u32[]{:S(2)}) copy-start(bf16[1,128,2048]{2,1,0:T(8,128)(2,1)} %param.9) | copy-start | bytes 1572868
  91.9 3.1 copy-start.16
  92.0 3.0 collective-permute-start.2
  98.5 4.5 copy-start
  99.4 5.6 %collective-permute-start.3 = (f32[16,128,128]{2,1,0:T(8,128)S(1)}, f32[16,128,128]{2,1,0:T(8,128)S(1)}, u32[]{:S(2)}, u32[]{:S(2)}) collective-permute-start(f32[16,128,128]{2,1,0:T(8,128)S(1)} %fusion.57), channel_id=1, source_target_pairs={{0,2},{2,4},{4,6},{6,8},{8,10},{10,12},{12,14},{1,3},{3,5},{5,7},{... | collective-permute-start | bytes 3145736 | tf_op jit(solution)/shard_map/ppermute | solution.py:13
  103.1 6.3 %collective-permute-start.9 = (f32[16,128,128]{2,1,0:T(8,128)S(1)}, f32[16,128,128]{2,1,0:T(8,128)S(1)}, u32[]{:S(2)}, u32[]{:S(2)}) collective-permute-start(f32[16,128,128]{2,1,0:T(8,128)S(1)} %fusion.55), channel_id=1, source_target_pairs={{2,0},{4,2},{6,4},{8,6},{10,8},{12,10},{14,12},{3,1},{5,3},{7,5},{... | collective-permute-start | bytes 3145736 | tf_op jit(solution)/shard_map/ppermute | solution.py:13
  109.9 36.4 %collective-permute-start.10 = (f32[16,128,128]{2,1,0:T(8,128)S(1)}, f32[16,128,128]{2,1,0:T(8,128)S(1)}, u32[]{:S(2)}, u32[]{:S(2)}) collective-permute-start(f32[16,128,128]{2,1,0:T(8,128)S(1)} %get-tuple-element.66), channel_id=1, source_target_pairs={{4,0},{6,2},{8,4},{10,6},{12,8},{14,10},{5,1},{7,3},{9,5},{11,7},{... | collective-permute-start | bytes 3145736 | tf_op jit(solution)/shard_map/ppermute | solution.py:13
  111.2 37.6 %collective-permute-start.4 = (f32[16,128,128]{2,1,0:T(8,128)S(1)}, f32[16,128,128]{2,1,0:T(8,128)S(1)}, u32[]{:S(2)}, u32[]{:S(2)}) collective-permute-start(f32[16,128,128]{2,1,0:T(8,128)S(1)} %get-tuple-element.65), channel_id=1, source_target_pairs={{0,4},{2,6},{4,8},{6,10},{8,12},{10,14},{1,5},{3,7},{5,9},{7,11},{... | collective-permute-start | bytes 3145736 | tf_op jit(solution)/shard_map/ppermute | solution.py:13
  125.6 4.9 collective-permute-start
  129.3 3.1 collective-permute-start.7
  147.6 53.6 %collective-permute-start.11 = (f32[16,128,128]{2,1,0:T(8,128)}, f32[16,128,128]{2,1,0:T(8,128)}, u32[]{:S(2)}, u32[]{:S(2)}) collective-permute-start(f32[16,128,128]{2,1,0:T(8,128)} %multiply_add_fusion.7), channel_id=1, source_target_pairs={{8,0},{10,2},{12,4},{14,6},{9,1},{11,3},{13,5},{15,7},{24,16},{26,... | collective-permute-start | bytes 3145736 | tf_op jit(solution)/shard_map/ppermute | solution.py:13
  150.0 54.3 %collective-permute-start.5 = (f32[16,128,128]{2,1,0:T(8,128)}, f32[16,128,128]{2,1,0:T(8,128)}, u32[]{:S(2)}, u32[]{:S(2)}) collective-permute-start(f32[16,128,128]{2,1,0:T(8,128)} %multiply_add_fusion.10), channel_id=1, source_target_pairs={{0,8},{2,10},{4,12},{6,14},{1,9},{3,11},{5,13},{7,15},{16,24},{18,... | collective-permute-start | bytes 3145736 | tf_op jit(solution)/shard_map/ppermute | solution.py:13
  162.8 19.2 %collective-permute-start.1 = (f32[16]{0:T(128)S(1)}, f32[16]{0:T(128)S(1)}, u32[]{:S(2)}, u32[]{:S(2)}) collective-permute-start(f32[16]{0:T(128)S(1)} %get-tuple-element.63), channel_id=1, source_target_pairs={{0,4},{2,6},{4,8},{6,10},{8,12},{10,14},{1,5},{3,7},{5,9},{7,11},{... | collective-permute-start | bytes 200 | tf_op jit(solution)/shard_map/ppermute | solution.py:13
  166.8 15.2 %collective-permute-start.8 = (f32[16]{0:T(128)S(1)}, f32[16]{0:T(128)S(1)}, u32[]{:S(2)}, u32[]{:S(2)}) collective-permute-start(f32[16]{0:T(128)S(1)} %get-tuple-element.64), channel_id=1, source_target_pairs={{4,0},{6,2},{8,4},{10,6},{12,8},{14,10},{5,1},{7,3},{9,5},{11,7},{... | collective-permute-start | bytes 200 | tf_op jit(solution)/shard_map/ppermute | solution.py:13
  187.1 22.2 %copy-start.19 = (bf16[16,128,128]{2,1,0:T(8,128)(2,1)}, bf16[16,128,128]{2,1,0:T(8,128)(2,1)S(1)}, u32[]{:S(2)}) copy-start(bf16[16,128,128]{2,1,0:T(8,128)(2,1)S(1)} %fusion.18) | copy-start | bytes 1572868
  202.9 6.4 %copy-start.1 = (bf16[16,16,8,128]{3,2,1,0:T(8,128)(2,1)S(1)}, bf16[16,16,8,128]{3,2,1,0:T(8,128)(2,1)}, u32[]{:S(2)}) copy-start(bf16[16,16,8,128]{3,2,1,0:T(8,128)(2,1)} %copy-done) | copy-start | bytes 1572868
  202.9 6.9 %collective-permute-start.12 = (bf16[16,128,128]{2,1,0:T(8,128)(2,1)S(1)}, bf16[16,128,128]{2,1,0:T(8,128)(2,1)S(1)}, u32[]{:S(2)}, u32[]{:S(2)}) collective-permute-start(bf16[16,128,128]{2,1,0:T(8,128)(2,1)S(1)} %multiply_add_fusion.6), channel_id=1, source_target_pairs={{2,0},{4,2},{6,4},{8,6},{10,8},{12,10},{14,12},{3,1},{5,3},{7,5},{... | collective-permute-start | bytes 1572872 | tf_op jit(solution)/shard_map/ppermute | solution.py:13
  206.1 3.8 copy-start.8
  206.1 4.7 collective-permute-start.6
  212.6 73.1 %copy-start.6 = (bf16[128,16,128]{0,2,1:T(8,128)(2,1)}, bf16[128,16,128]{0,2,1:T(8,128)(2,1)S(1)}, u32[]{:S(2)}) copy-start(bf16[128,16,128]{0,2,1:T(8,128)(2,1)S(1)} %get-tuple-element.36) | copy-start | bytes 1572868
  213.6 18.2 %collective-permute-start.13 = (f32[16,128,128]{2,1,0:T(8,128)S(1)}, f32[16,128,128]{2,1,0:T(8,128)S(1)}, u32[]{:S(2)}, u32[]{:S(2)}) collective-permute-start(f32[16,128,128]{2,1,0:T(8,128)S(1)} %fusion.53), channel_id=1, source_target_pairs={{0,2},{2,4},{4,6},{6,8},{8,10},{10,12},{12,14},{1,3},{3,5},{5,7},{... | collective-permute-start | bytes 3145736 | tf_op jit(solution)/shard_map/ppermute | solution.py:13
  229.6 6.5 %collective-permute-start.17 = (f32[16,128,128]{2,1,0:T(8,128)S(1)}, f32[16,128,128]{2,1,0:T(8,128)S(1)}, u32[]{:S(2)}, u32[]{:S(2)}) collective-permute-start(f32[16,128,128]{2,1,0:T(8,128)S(1)} %fusion.51), channel_id=1, source_target_pairs={{2,0},{4,2},{6,4},{8,6},{10,8},{12,10},{14,12},{3,1},{5,3},{7,5},{... | collective-permute-start | bytes 3145736 | tf_op jit(solution)/shard_map/ppermute | solution.py:13
  236.7 35.7 %collective-permute-start.18 = (f32[16,128,128]{2,1,0:T(8,128)S(1)}, f32[16,128,128]{2,1,0:T(8,128)S(1)}, u32[]{:S(2)}, u32[]{:S(2)}) collective-permute-start(f32[16,128,128]{2,1,0:T(8,128)S(1)} %get-tuple-element.62), channel_id=1, source_target_pairs={{4,0},{6,2},{8,4},{10,6},{12,8},{14,10},{5,1},{7,3},{9,5},{11,7},{... | collective-permute-start | bytes 3145736 | tf_op jit(solution)/shard_map/ppermute | solution.py:13
  238.0 37.1 %collective-permute-start.14 = (f32[16,128,128]{2,1,0:T(8,128)S(1)}, f32[16,128,128]{2,1,0:T(8,128)S(1)}, u32[]{:S(2)}, u32[]{:S(2)}) collective-permute-start(f32[16,128,128]{2,1,0:T(8,128)S(1)} %get-tuple-element.61), channel_id=1, source_target_pairs={{0,4},{2,6},{4,8},{6,10},{8,12},{10,14},{1,5},{3,7},{5,9},{7,11},{... | collective-permute-start | bytes 3145736 | tf_op jit(solution)/shard_map/ppermute | solution.py:13
  253.1 32.1 %copy-start.21 = (bf16[16,128,128]{2,1,0:T(8,128)(2,1)}, bf16[16,128,128]{2,1,0:T(8,128)(2,1)S(1)}, u32[]{:S(2)}) copy-start(bf16[16,128,128]{2,1,0:T(8,128)(2,1)S(1)} %fusion.19) | copy-start | bytes 1572868
  273.6 11.6 %copy-start.4 = (bf16[128,2048]{0,1:T(8,128)(2,1)S(1)}, bf16[128,2048]{0,1:T(8,128)(2,1)}, u32[]{:S(2)}) copy-start(bf16[128,2048]{0,1:T(8,128)(2,1)} %copy.97) | copy-start | bytes 1572868
  273.6 53.3 %collective-permute-start.19 = (f32[16,128,128]{2,1,0:T(8,128)}, f32[16,128,128]{2,1,0:T(8,128)}, u32[]{:S(2)}, u32[]{:S(2)}) collective-permute-start(f32[16,128,128]{2,1,0:T(8,128)} %multiply_add_fusion.1), channel_id=1, source_target_pairs={{8,0},{10,2},{12,4},{14,6},{9,1},{11,3},{13,5},{15,7},{24,16},{26,... | collective-permute-start | bytes 3145736 | tf_op jit(solution)/shard_map/ppermute | solution.py:13
  276.2 53.9 %collective-permute-start.15 = (f32[16,128,128]{2,1,0:T(8,128)}, f32[16,128,128]{2,1,0:T(8,128)}, u32[]{:S(2)}, u32[]{:S(2)}) collective-permute-start(f32[16,128,128]{2,1,0:T(8,128)} %multiply_add_fusion.4), channel_id=1, source_target_pairs={{0,8},{2,10},{4,12},{6,14},{1,9},{3,11},{5,13},{7,15},{16,24},{18,... | collective-permute-start | bytes 3145736 | tf_op jit(solution)/shard_map/ppermute | solution.py:13
  328.6 6.4 %copy-start.7 = (bf16[128,16,128]{0,2,1:T(8,128)(2,1)S(1)}, bf16[128,16,128]{0,2,1:T(8,128)(2,1)}, u32[]{:S(2)}) copy-start(bf16[128,16,128]{0,2,1:T(8,128)(2,1)} %copy-done.6) | copy-start | bytes 1572868
  328.6 6.4 %copy-start.20 = (bf16[16,128,128]{2,1,0:T(8,128)(2,1)S(1)}, bf16[16,128,128]{2,1,0:T(8,128)(2,1)}, u32[]{:S(2)}) copy-start(bf16[16,128,128]{2,1,0:T(8,128)(2,1)} %copy-done.19) | copy-start | bytes 1572868
  328.6 7.8 %collective-permute-start.20 = (bf16[16,128,128]{2,1,0:T(8,128)(2,1)S(1)}, bf16[16,128,128]{2,1,0:T(8,128)(2,1)S(1)}, u32[]{:S(2)}, u32[]{:S(2)}) collective-permute-start(bf16[16,128,128]{2,1,0:T(8,128)(2,1)S(1)} %multiply_add_fusion), channel_id=1, source_target_pairs={{2,0},{4,2},{6,4},{8,6},{10,8},{12,10},{14,12},{3,1},{5,3},{7,5},{... | collective-permute-start | bytes 1572872 | tf_op jit(solution)/shard_map/ppermute | solution.py:13
  331.8 4.6 copy-start.2
  331.8 5.1 collective-permute-start.16
  336.4 2.2 copy-start.22
  340.6 1.7 copy-start.5
  340.6 1.7 copy-start.14
  340.6 1.8 copy-start.18
  346.8 8.2 %collective-permute-start.21 = (bf16[3,3,2048]{2,1,0:T(4,128)(2,1)S(1)}, bf16[3,3,2048]{2,1,0:T(4,128)(2,1)S(1)}, u32[]{:S(2)}, u32[]{:S(2)}) collective-permute-start(bf16[3,3,2048]{2,1,0:T(4,128)(2,1)S(1)} %pad_maximum_fusion.3), channel_id=1, source_target_pairs={{2,0},{4,2},{6,4},{8,6},{10,8},{12,10},{14,12},{3,1},{5,3},{7,5},{... | collective-permute-start | bytes 110600 | tf_op jit(solution)/shard_map/ppermute | solution.py:13
  359.4 178.6 %all-reduce.2.cloned.1.call-start = ((), (), s32[]{:S(2)}) async-start(), calls=%async_computation.3 | async-start | bytes 196608 | tf_op jit(solution)/shard_map/psum | solution.py:253
  361.5 31.9 %copy-start.11 = (f32[128,16,128]{0,2,1:T(8,128)S(1)}, f32[128,16,128]{0,2,1:T(8,128)}, u32[]{:S(2)}) copy-start(f32[128,16,128]{0,2,1:T(8,128)} %get-tuple-element.74) | copy-start | bytes 3145732
  394.7 2.1 copy-start.12
  398.2 4.2 copy-start.13
  402.4 2.5 copy-start.10
  404.9 41.8 %copy-start.25 = (bf16[16,128,128]{2,1,0:T(8,128)(2,1)S(1)}, bf16[16,128,128]{2,1,0:T(8,128)(2,1)}, u32[]{:S(2)}) copy-start(bf16[16,128,128]{2,1,0:T(8,128)(2,1)} %copy.130) | copy-start | bytes 1572868
  (3 other events, 3.9 us)
Sparse Core Ops, SparseCore 0:
  10.2 76.9 all-gather.2
  359.6 87.0 all-gather.4
  450.7 87.3 all-reduce.1
where the time goes:
time: 548 us; the launch traced here: 546 us
  waiting for transfers between devices  309 us (56%)
  starting transfers between devices  98.8 us (18%)
  matrix products  34.2 us (6%)
  other arithmetic  30.6 us (6%)
  blocking collectives  29.8 us (5%)
  local copies, waits for them, and re-layouts  29.6 us (5%)
  between operations  14.4 us (3%)
    ppermute x22, waiting for transfers between devices, shifted(): return lax.ppermute(block, axis, route)  115 us
    ppermute x22, starting transfers between devices, shifted(): return lax.ppermute(block, axis, route)  98.7 us
    psum x1, waiting for transfers between devices, local(): grad_conv = lax.psum(kernel_terms, ('seq', 'rep'))  84.3 us
    all_gather x1, waiting for transfers between devices, local(): lax.all_gather(value_weight, ('seq', 'rep'), axis=0, tiled=True)  75.3 us
    all_gather x1, waiting for transfers between devices, local(): lax.all_gather(grad_value, ('seq', 'rep'), axis=0, tiled=True)  33.6 us
    all_to_all x1, blocking collectives, local(): feature_rows = lax.all_to_all(gathered, ('seq', 'rep'), 1, 0, tiled=True)  29.8 us
    add x10, other arithmetic, chain_join(): following[0][:, None, None] * earlier[1] + following[1]  12.7 us
  transfers between devices with their start and end apart: 25, of which 16 were waited for; matrix products, arithmetic and copies ran while one was open for 12% of the time, Pallas kernels for 0%

commit v1 on v0

--- a/solution.py
+++ b/solution.py
@@ -250,7 +250,7 @@
         )
         * grad_scale
     )
-    grad_conv = lax.psum(kernel_terms, ("seq", "rep"))
+    grad_conv = jnp.sum(lax.all_gather(kernel_terms, ("seq", "rep")), axis=0)
     partial_x = lax.dot_general(
         grad_value,
         lax.all_gather(value_weight, ("seq", "rep"), axis=0, tiled=True),

time: 548 us -> 505 us (0.922)
  waiting for transfers between devices: 309 us -> 271 us
    psum x1 -> x0, waiting for transfers between devices: 84.3 us -> none  [local(): grad_conv = lax.psum(kernel_terms, ('seq', 'rep'))]
    all_gather x1, waiting for transfers between devices: 33.6 us -> 73.5 us  [local(): lax.all_gather(grad_value, ('seq', 'rep'), axis=0, tiled=True)]
    all_gather x0 -> x1, waiting for transfers between devices: none -> 10 us  [local(): grad_conv = jnp.sum(lax.all_gather(kernel_terms, ('seq', 'rep')), axis=0)]
  transfers between devices with their start and end apart: 25 -> 25, of which waited for: 16 -> 15; matrix products, arithmetic and copies ran while one was open for 12% -> 10% of each run, Pallas kernels for 0% -> 0%
where the time goes in v1:
time: 505 us; the launch traced here: 503 us
  waiting for transfers between devices  271 us (54%)
  starting transfers between devices  98.8 us (20%)
  matrix products  33.2 us (7%)
  other arithmetic  30.5 us (6%)
  blocking collectives  29.9 us (6%)
  local copies, waits for them, and re-layouts  25.8 us (5%)
  between operations  14.5 us (3%)
    ppermute x22, waiting for transfers between devices, shifted(): return lax.ppermute(block, axis, route)  110 us
    ppermute x22, starting transfers between devices, shifted(): return lax.ppermute(block, axis, route)  98.7 us
    all_gather x1, waiting for transfers between devices, local(): lax.all_gather(value_weight, ('seq', 'rep'), axis=0, tiled=True)  75.4 us
    all_gather x1, waiting for transfers between devices, local(): lax.all_gather(grad_value, ('seq', 'rep'), axis=0, tiled=True)  73.5 us
    all_to_all x1, blocking collectives, local(): feature_rows = lax.all_to_all(gathered, ('seq', 'rep'), 1, 0, tiled=True)  29.9 us
    add x10, other arithmetic, chain_join(): following[0][:, None, None] * earlier[1] + following[1]  12.7 us
  transfers between devices with their start and end apart: 25, of which 15 were waited for; matrix products, arithmetic and copies ran while one was open for 10% of the time, Pallas kernels for 0%

profile of v1, /device:TPU:0, one launch (start us, length us, event | category | flops | bytes accessed | tf_op | source)
XLA Modules:
  0.0 503.4 jit_solution(15200036045377254061)
XLA Ops:
  11.8 75.4 %all-gather.4.cloned.1.call-done = bf16[2048,2048]{1,0:T(8,128)(2,1)} async-done(((bf16[128,2048]{1,0:T(8,128)(2,1)}), bf16[2048,2048]{1,0:T(8,128)(2,1)}) %all-gather.4.cloned.1.call-update) | async-done | bytes 8388624 | tf_op jit(solution)/shard_map/all_gather | solution.py:118
  87.2 4.6 convolution_convert_fusion.1
  92.0 2.2 collective-permute-start.2
  99.4 3.4 collective-permute-start.3
  105.0 4.4 collective-permute-done.9
  111.2 14.4 %collective-permute-start.4 = (f32[16,128,128]{2,1,0:T(8,128)S(1)}, f32[16,128,128]{2,1,0:T(8,128)S(1)}, u32[]{:S(2)}, u32[]{:S(2)}) collective-permute-start(f32[16,128,128]{2,1,0:T(8,128)S(1)} %get-tuple-element.71), channel_id=1, source_target_pairs={{0,4},{2,6},{4,8},{6,10},{8,12},{10,14},{1,5},{3,7},{5,9},{7,11},{... | collective-permute-start | bytes 3145736 | tf_op jit(solution)/shard_map/ppermute | solution.py:13
  125.6 3.6 collective-permute-start
  130.6 1.7 collective-permute-done.7
  132.3 14.0 %collective-permute-done.10 = f32[16,128,128]{2,1,0:T(8,128)S(1)} collective-permute-done((f32[16,128,128]{2,1,0:T(8,128)S(1)}, f32[16,128,128]{2,1,0:T(8,128)S(1)}, u32[]{:S(2)}, u32[]{:S(2)}) %collective-permute-start.10) | collective-permute-done | bytes 1048608 | tf_op jit(solution)/shard_map/ppermute | solution.py:13
  150.0 10.6 %collective-permute-start.5 = (f32[16,128,128]{2,1,0:T(8,128)}, f32[16,128,128]{2,1,0:T(8,128)}, u32[]{:S(2)}, u32[]{:S(2)}) collective-permute-start(f32[16,128,128]{2,1,0:T(8,128)} %multiply_add_fusion.10), channel_id=1, source_target_pairs={{0,8},{2,10},{4,12},{6,14},{1,9},{3,11},{5,13},{7,15},{16,24},{18,... | collective-permute-start | bytes 3145736 | tf_op jit(solution)/shard_map/ppermute | solution.py:13
  160.6 2.2 copy.152
  162.8 4.0 collective-permute-start.1
  168.1 13.9 %collective-permute-done.1 = f32[16]{0:T(128)S(1)} collective-permute-done((f32[16]{0:T(128)S(1)}, f32[16]{0:T(128)S(1)}, u32[]{:S(2)}, u32[]{:S(2)}) %collective-permute-start.1) | collective-permute-done | bytes 96 | tf_op jit(solution)/shard_map/ppermute | solution.py:13
  183.3 2.0 copy.143
  185.3 1.7 fusion.18
  187.1 14.1 %collective-permute-done.11 = f32[16,128,128]{2,1,0:T(8,128)} collective-permute-done((f32[16,128,128]{2,1,0:T(8,128)}, f32[16,128,128]{2,1,0:T(8,128)}, u32[]{:S(2)}, u32[]{:S(2)}) %collective-permute-start.11) | collective-permute-done | bytes 1048608 | tf_op jit(solution)/shard_map/ppermute | solution.py:13
  201.1 1.7 multiply_add_fusion.6
  204.3 1.7 multiply_add_fusion.9
  206.1 3.2 collective-permute-start.6
  213.6 16.0 %collective-permute-start.13 = (f32[16,128,128]{2,1,0:T(8,128)S(1)}, f32[16,128,128]{2,1,0:T(8,128)S(1)}, u32[]{:S(2)}, u32[]{:S(2)}) collective-permute-start(f32[16,128,128]{2,1,0:T(8,128)S(1)} %fusion.53), channel_id=1, source_target_pairs={{0,2},{2,4},{4,6},{6,8},{8,10},{10,12},{12,14},{1,3},{3,5},{5,7},{... | collective-permute-start | bytes 3145736 | tf_op jit(solution)/shard_map/ppermute | solution.py:13
  231.8 4.3 collective-permute-done.17
  238.0 14.6 %collective-permute-start.14 = (f32[16,128,128]{2,1,0:T(8,128)S(1)}, f32[16,128,128]{2,1,0:T(8,128)S(1)}, u32[]{:S(2)}, u32[]{:S(2)}) collective-permute-start(f32[16,128,128]{2,1,0:T(8,128)S(1)} %get-tuple-element.67), channel_id=1, source_target_pairs={{0,4},{2,6},{4,8},{6,10},{8,12},{10,14},{1,5},{3,7},{5,9},{7,11},{... | collective-permute-start | bytes 3145736 | tf_op jit(solution)/shard_map/ppermute | solution.py:13
  253.4 19.0 %collective-permute-done.18 = f32[16,128,128]{2,1,0:T(8,128)S(1)} collective-permute-done((f32[16,128,128]{2,1,0:T(8,128)S(1)}, f32[16,128,128]{2,1,0:T(8,128)S(1)}, u32[]{:S(2)}, u32[]{:S(2)}) %collective-permute-start.18) | collective-permute-done | bytes 1048608 | tf_op jit(solution)/shard_map/ppermute | solution.py:13
  276.2 9.0 %collective-permute-start.15 = (f32[16,128,128]{2,1,0:T(8,128)}, f32[16,128,128]{2,1,0:T(8,128)}, u32[]{:S(2)}, u32[]{:S(2)}) collective-permute-start(f32[16,128,128]{2,1,0:T(8,128)} %multiply_add_fusion.4), channel_id=1, source_target_pairs={{0,8},{2,10},{4,12},{6,14},{1,9},{3,11},{5,13},{7,15},{16,24},{18,... | collective-permute-start | bytes 3145736 | tf_op jit(solution)/shard_map/ppermute | solution.py:13
  285.7 1.5 fusion.91
  287.2 2.0 copy.200
  289.3 1.5 convolution_bitcast_fusion.3
  290.8 36.1 %collective-permute-done.19 = f32[16,128,128]{2,1,0:T(8,128)} collective-permute-done((f32[16,128,128]{2,1,0:T(8,128)}, f32[16,128,128]{2,1,0:T(8,128)}, u32[]{:S(2)}, u32[]{:S(2)}) %collective-permute-start.19) | collective-permute-done | bytes 1048608 | tf_op jit(solution)/shard_map/ppermute | solution.py:13
  326.9 1.7 multiply_add_fusion
  330.1 1.7 multiply_add_fusion.3
  331.8 3.2 collective-permute-start.16
  336.8 1.7 fusion.90
  338.5 2.1 copy.201
  340.6 1.7 fusion.2
  342.4 1.5 fusion.89
  343.9 2.0 copy.202
  348.1 2.5 copy.157
  350.6 2.5 copy.170
  353.2 2.6 copy.203
  355.8 4.3 multiply_reduce_fusion.11
  360.1 1.7 multiply_reduce_fusion.7
  361.9 1.7 multiply_reduce_fusion.3
  365.5 29.9 %all_to_all.19 = bf16[128,16,128]{0,2,1:T(8,128)(2,1)S(1)} all-to-all(bf16[128,16,128]{0,2,1:T(8,128)(2,1)S(1)} %bitcast.200), channel_id=1, replica_groups=mesh['parts'=2,'seq'=8,'rep'=2,'head'=1] {'seq','rep'}, dimensions={1} | all-to-all | bytes 1048576 | tf_op jit(solution)/shard_map/all_to_all | solution.py:263
  396.7 7.3 %fusion.1 = bf16[1,128,2048]{2,1,0:T(8,128)(2,1)} fusion(bf16[128,2048]{1,0:T(8,128)(2,1)S(1)} %copy-done.10, bf16[2048,2048]{1,0:T(8,128)(2,1)} %all-gather.4.cloned.1.call-done), kind=kOutput, calls=%fused_computation.4 | convolution fusion | flops 1074003968 | bytes 9437184 | tf_op jit(solution)/shard_map/dot_general | solution.py:254
  404.0 10.0 %all-gather.8.cloned.1.call-done = f32[16,3,4,2048]{3,2,1,0:T(4,128)} async-done(((f32[1,3,4,2048]{3,2,1,0:T(4,128)}), f32[16,3,4,2048]{3,2,1,0:T(4,128)}) %all-gather.8.cloned.1.call-update) | async-done | bytes 1572880 | tf_op jit(solution)/shard_map/all_gather | solution.py:253
  414.0 2.4 reduce_sum.149
  416.3 73.5 %all-gather.6.cloned.1.call-done = bf16[2048,2048]{1,0:T(8,128)(2,1)} async-done(((bf16[128,2048]{1,0:T(8,128)(2,1)}), bf16[2048,2048]{1,0:T(8,128)(2,1)}) %all-gather.6.cloned.1.call-update) | async-done | bytes 8388624 | tf_op jit(solution)/shard_map/all_gather | solution.py:264
  489.8 5.8 %fusion = f32[128,2048]{0,1:T(8,128)S(1)} fusion(bf16[2048,2048]{1,0:T(8,128)(2,1)} %all-gather.6.cloned.1.call-done, bf16[2048,128]{1,0:T(8,128)(2,1)S(1)} %bitcast.204), kind=kOutput, calls=%fused_computation.1 | convolution fusion | flops 1074003968 | bytes 9961472 | tf_op jit(solution)/shard_map/dot_general | solution.py:266
  (135 shorter events, 46.1 us)
Async XLA Ops:
  7.2 80.1 %copy-start.14 = (bf16[1,128,2048]{2,1,0:T(8,128)(2,1)S(1)}, bf16[1,128,2048]{2,1,0:T(8,128)(2,1)}, u32[]{:S(2)}) copy-start(bf16[1,128,2048]{2,1,0:T(8,128)(2,1)} %param.7) | copy-start | bytes 1572868
  7.2 80.1 %all-gather.4.cloned.1.call-start = ((), (), s32[]{:S(2)}) async-start(), calls=%async_computation.1 | async-start | bytes 8912896 | tf_op jit(solution)/shard_map/all_gather | solution.py:118
  7.9 406.1 %all-gather.8.cloned.1.call-start = ((), (), s32[]{:S(2)}) async-start(), calls=%async_computation.3 | async-start | bytes 1671168 | tf_op jit(solution)/shard_map/all_gather | solution.py:253
  11.8 83.2 %copy-start.24 = (bf16[1,128,2048]{2,1,0:T(8,128)(2,1)S(1)}, bf16[1,128,2048]{2,1,0:T(8,128)(2,1)}, u32[]{:S(2)}) copy-start(bf16[1,128,2048]{2,1,0:T(8,128)(2,1)} %param.10) | copy-start | bytes 1572868
  11.8 83.2 %copy-start.25 = (bf16[1,128,2048]{2,1,0:T(8,128)(2,1)S(1)}, bf16[1,128,2048]{2,1,0:T(8,128)(2,1)}, u32[]{:S(2)}) copy-start(bf16[1,128,2048]{2,1,0:T(8,128)(2,1)} %param.9) | copy-start | bytes 1572868
  91.9 3.1 copy-start.16
  92.0 3.0 collective-permute-start.2
  98.5 4.5 copy-start
  99.4 5.6 %collective-permute-start.3 = (f32[16,128,128]{2,1,0:T(8,128)S(1)}, f32[16,128,128]{2,1,0:T(8,128)S(1)}, u32[]{:S(2)}, u32[]{:S(2)}) collective-permute-start(f32[16,128,128]{2,1,0:T(8,128)S(1)} %fusion.57), channel_id=1, source_target_pairs={{0,2},{2,4},{4,6},{6,8},{8,10},{10,12},{12,14},{1,3},{3,5},{5,7},{... | collective-permute-start | bytes 3145736 | tf_op jit(solution)/shard_map/ppermute | solution.py:13
  103.1 6.3 %collective-permute-start.9 = (f32[16,128,128]{2,1,0:T(8,128)S(1)}, f32[16,128,128]{2,1,0:T(8,128)S(1)}, u32[]{:S(2)}, u32[]{:S(2)}) collective-permute-start(f32[16,128,128]{2,1,0:T(8,128)S(1)} %fusion.55), channel_id=1, source_target_pairs={{2,0},{4,2},{6,4},{8,6},{10,8},{12,10},{14,12},{3,1},{5,3},{7,5},{... | collective-permute-start | bytes 3145736 | tf_op jit(solution)/shard_map/ppermute | solution.py:13
  109.9 36.4 %collective-permute-start.10 = (f32[16,128,128]{2,1,0:T(8,128)S(1)}, f32[16,128,128]{2,1,0:T(8,128)S(1)}, u32[]{:S(2)}, u32[]{:S(2)}) collective-permute-start(f32[16,128,128]{2,1,0:T(8,128)S(1)} %get-tuple-element.72), channel_id=1, source_target_pairs={{4,0},{6,2},{8,4},{10,6},{12,8},{14,10},{5,1},{7,3},{9,5},{11,7},{... | collective-permute-start | bytes 3145736 | tf_op jit(solution)/shard_map/ppermute | solution.py:13
  111.2 37.6 %collective-permute-start.4 = (f32[16,128,128]{2,1,0:T(8,128)S(1)}, f32[16,128,128]{2,1,0:T(8,128)S(1)}, u32[]{:S(2)}, u32[]{:S(2)}) collective-permute-start(f32[16,128,128]{2,1,0:T(8,128)S(1)} %get-tuple-element.71), channel_id=1, source_target_pairs={{0,4},{2,6},{4,8},{6,10},{8,12},{10,14},{1,5},{3,7},{5,9},{7,11},{... | collective-permute-start | bytes 3145736 | tf_op jit(solution)/shard_map/ppermute | solution.py:13
  125.6 4.9 collective-permute-start
  129.3 3.1 collective-permute-start.7
  147.5 53.6 %collective-permute-start.11 = (f32[16,128,128]{2,1,0:T(8,128)}, f32[16,128,128]{2,1,0:T(8,128)}, u32[]{:S(2)}, u32[]{:S(2)}) collective-permute-start(f32[16,128,128]{2,1,0:T(8,128)} %multiply_add_fusion.7), channel_id=1, source_target_pairs={{8,0},{10,2},{12,4},{14,6},{9,1},{11,3},{13,5},{15,7},{24,16},{26,... | collective-permute-start | bytes 3145736 | tf_op jit(solution)/shard_map/ppermute | solution.py:13
  150.0 54.3 %collective-permute-start.5 = (f32[16,128,128]{2,1,0:T(8,128)}, f32[16,128,128]{2,1,0:T(8,128)}, u32[]{:S(2)}, u32[]{:S(2)}) collective-permute-start(f32[16,128,128]{2,1,0:T(8,128)} %multiply_add_fusion.10), channel_id=1, source_target_pairs={{0,8},{2,10},{4,12},{6,14},{1,9},{3,11},{5,13},{7,15},{16,24},{18,... | collective-permute-start | bytes 3145736 | tf_op jit(solution)/shard_map/ppermute | solution.py:13
  162.8 19.2 %collective-permute-start.1 = (f32[16]{0:T(128)S(1)}, f32[16]{0:T(128)S(1)}, u32[]{:S(2)}, u32[]{:S(2)}) collective-permute-start(f32[16]{0:T(128)S(1)} %get-tuple-element.69), channel_id=1, source_target_pairs={{0,4},{2,6},{4,8},{6,10},{8,12},{10,14},{1,5},{3,7},{5,9},{7,11},{... | collective-permute-start | bytes 200 | tf_op jit(solution)/shard_map/ppermute | solution.py:13
  166.8 15.2 %collective-permute-start.8 = (f32[16]{0:T(128)S(1)}, f32[16]{0:T(128)S(1)}, u32[]{:S(2)}, u32[]{:S(2)}) collective-permute-start(f32[16]{0:T(128)S(1)} %get-tuple-element.70), channel_id=1, source_target_pairs={{4,0},{6,2},{8,4},{10,6},{12,8},{14,10},{5,1},{7,3},{9,5},{11,7},{... | collective-permute-start | bytes 200 | tf_op jit(solution)/shard_map/ppermute | solution.py:13
  187.1 22.2 %copy-start.20 = (bf16[16,128,128]{2,1,0:T(8,128)(2,1)}, bf16[16,128,128]{2,1,0:T(8,128)(2,1)S(1)}, u32[]{:S(2)}) copy-start(bf16[16,128,128]{2,1,0:T(8,128)(2,1)S(1)} %fusion.18) | copy-start | bytes 1572868
  202.9 6.4 %copy-start.1 = (bf16[16,16,8,128]{3,2,1,0:T(8,128)(2,1)S(1)}, bf16[16,16,8,128]{3,2,1,0:T(8,128)(2,1)}, u32[]{:S(2)}) copy-start(bf16[16,16,8,128]{3,2,1,0:T(8,128)(2,1)} %copy-done) | copy-start | bytes 1572868
  202.9 6.9 %collective-permute-start.12 = (bf16[16,128,128]{2,1,0:T(8,128)(2,1)S(1)}, bf16[16,128,128]{2,1,0:T(8,128)(2,1)S(1)}, u32[]{:S(2)}, u32[]{:S(2)}) collective-permute-start(bf16[16,128,128]{2,1,0:T(8,128)(2,1)S(1)} %multiply_add_fusion.6), channel_id=1, source_target_pairs={{2,0},{4,2},{6,4},{8,6},{10,8},{12,10},{14,12},{3,1},{5,3},{7,5},{... | collective-permute-start | bytes 1572872 | tf_op jit(solution)/shard_map/ppermute | solution.py:13
  206.1 3.8 copy-start.8
  206.1 4.7 collective-permute-start.6
  212.6 73.1 %copy-start.6 = (bf16[128,16,128]{0,2,1:T(8,128)(2,1)}, bf16[128,16,128]{0,2,1:T(8,128)(2,1)S(1)}, u32[]{:S(2)}) copy-start(bf16[128,16,128]{0,2,1:T(8,128)(2,1)S(1)} %get-tuple-element.42) | copy-start | bytes 1572868
  213.6 18.2 %collective-permute-start.13 = (f32[16,128,128]{2,1,0:T(8,128)S(1)}, f32[16,128,128]{2,1,0:T(8,128)S(1)}, u32[]{:S(2)}, u32[]{:S(2)}) collective-permute-start(f32[16,128,128]{2,1,0:T(8,128)S(1)} %fusion.53), channel_id=1, source_target_pairs={{0,2},{2,4},{4,6},{6,8},{8,10},{10,12},{12,14},{1,3},{3,5},{5,7},{... | collective-permute-start | bytes 3145736 | tf_op jit(solution)/shard_map/ppermute | solution.py:13
  229.6 6.5 %collective-permute-start.17 = (f32[16,128,128]{2,1,0:T(8,128)S(1)}, f32[16,128,128]{2,1,0:T(8,128)S(1)}, u32[]{:S(2)}, u32[]{:S(2)}) collective-permute-start(f32[16,128,128]{2,1,0:T(8,128)S(1)} %fusion.51), channel_id=1, source_target_pairs={{2,0},{4,2},{6,4},{8,6},{10,8},{12,10},{14,12},{3,1},{5,3},{7,5},{... | collective-permute-start | bytes 3145736 | tf_op jit(solution)/shard_map/ppermute | solution.py:13
  236.7 35.7 %collective-permute-start.18 = (f32[16,128,128]{2,1,0:T(8,128)S(1)}, f32[16,128,128]{2,1,0:T(8,128)S(1)}, u32[]{:S(2)}, u32[]{:S(2)}) collective-permute-start(f32[16,128,128]{2,1,0:T(8,128)S(1)} %get-tuple-element.68), channel_id=1, source_target_pairs={{4,0},{6,2},{8,4},{10,6},{12,8},{14,10},{5,1},{7,3},{9,5},{11,7},{... | collective-permute-start | bytes 3145736 | tf_op jit(solution)/shard_map/ppermute | solution.py:13
  238.0 37.1 %collective-permute-start.14 = (f32[16,128,128]{2,1,0:T(8,128)S(1)}, f32[16,128,128]{2,1,0:T(8,128)S(1)}, u32[]{:S(2)}, u32[]{:S(2)}) collective-permute-start(f32[16,128,128]{2,1,0:T(8,128)S(1)} %get-tuple-element.67), channel_id=1, source_target_pairs={{0,4},{2,6},{4,8},{6,10},{8,12},{10,14},{1,5},{3,7},{5,9},{7,11},{... | collective-permute-start | bytes 3145736 | tf_op jit(solution)/shard_map/ppermute | solution.py:13
  253.1 32.1 %copy-start.22 = (bf16[16,128,128]{2,1,0:T(8,128)(2,1)}, bf16[16,128,128]{2,1,0:T(8,128)(2,1)S(1)}, u32[]{:S(2)}) copy-start(bf16[16,128,128]{2,1,0:T(8,128)(2,1)S(1)} %fusion.19) | copy-start | bytes 1572868
  273.6 11.6 %copy-start.4 = (bf16[128,2048]{0,1:T(8,128)(2,1)S(1)}, bf16[128,2048]{0,1:T(8,128)(2,1)}, u32[]{:S(2)}) copy-start(bf16[128,2048]{0,1:T(8,128)(2,1)} %copy.141) | copy-start | bytes 1572868
  273.6 53.3 %collective-permute-start.19 = (f32[16,128,128]{2,1,0:T(8,128)}, f32[16,128,128]{2,1,0:T(8,128)}, u32[]{:S(2)}, u32[]{:S(2)}) collective-permute-start(f32[16,128,128]{2,1,0:T(8,128)} %multiply_add_fusion.1), channel_id=1, source_target_pairs={{8,0},{10,2},{12,4},{14,6},{9,1},{11,3},{13,5},{15,7},{24,16},{26,... | collective-permute-start | bytes 3145736 | tf_op jit(solution)/shard_map/ppermute | solution.py:13
  276.2 53.9 %collective-permute-start.15 = (f32[16,128,128]{2,1,0:T(8,128)}, f32[16,128,128]{2,1,0:T(8,128)}, u32[]{:S(2)}, u32[]{:S(2)}) collective-permute-start(f32[16,128,128]{2,1,0:T(8,128)} %multiply_add_fusion.4), channel_id=1, source_target_pairs={{0,8},{2,10},{4,12},{6,14},{1,9},{3,11},{5,13},{7,15},{16,24},{18,... | collective-permute-start | bytes 3145736 | tf_op jit(solution)/shard_map/ppermute | solution.py:13
  328.6 6.4 %copy-start.7 = (bf16[128,16,128]{0,2,1:T(8,128)(2,1)S(1)}, bf16[128,16,128]{0,2,1:T(8,128)(2,1)}, u32[]{:S(2)}) copy-start(bf16[128,16,128]{0,2,1:T(8,128)(2,1)} %copy-done.6) | copy-start | bytes 1572868
  328.6 6.4 %copy-start.21 = (bf16[16,128,128]{2,1,0:T(8,128)(2,1)S(1)}, bf16[16,128,128]{2,1,0:T(8,128)(2,1)}, u32[]{:S(2)}) copy-start(bf16[16,128,128]{2,1,0:T(8,128)(2,1)} %copy-done.20) | copy-start | bytes 1572868
  328.6 7.7 %collective-permute-start.20 = (bf16[16,128,128]{2,1,0:T(8,128)(2,1)S(1)}, bf16[16,128,128]{2,1,0:T(8,128)(2,1)S(1)}, u32[]{:S(2)}, u32[]{:S(2)}) collective-permute-start(bf16[16,128,128]{2,1,0:T(8,128)(2,1)S(1)} %multiply_add_fusion), channel_id=1, source_target_pairs={{2,0},{4,2},{6,4},{8,6},{10,8},{12,10},{14,12},{3,1},{5,3},{7,5},{... | collective-permute-start | bytes 1572872 | tf_op jit(solution)/shard_map/ppermute | solution.py:13
  331.8 4.5 copy-start.2
  331.8 5.0 collective-permute-start.16
  336.3 2.2 copy-start.23
  336.8 1.7 copy-start.17
  340.6 1.7 copy-start.5
  340.6 1.7 copy-start.13
  340.6 1.8 copy-start.18
  346.8 9.0 %collective-permute-start.21 = (bf16[3,3,2048]{2,1,0:T(4,128)(2,1)S(1)}, bf16[3,3,2048]{2,1,0:T(4,128)(2,1)S(1)}, u32[]{:S(2)}, u32[]{:S(2)}) collective-permute-start(bf16[3,3,2048]{2,1,0:T(4,128)(2,1)S(1)} %pad_maximum_fusion.3), channel_id=1, source_target_pairs={{2,0},{4,2},{6,4},{8,6},{10,8},{12,10},{14,12},{3,1},{5,3},{7,5},{... | collective-permute-start | bytes 110600 | tf_op jit(solution)/shard_map/ppermute | solution.py:13
  355.8 4.3 copy-start.12
  360.1 1.7 copy-start.11
  363.6 1.6 copy-start.15
  364.4 125.4 %all-gather.6.cloned.1.call-start = ((), (), s32[]{:S(2)}) async-start(), calls=%async_computation.2 | async-start | bytes 8912896 | tf_op jit(solution)/shard_map/all_gather | solution.py:264
  365.4 30.2 %copy-start.19 = (bf16[128,16,128]{0,2,1:T(8,128)(2,1)S(1)}, bf16[128,16,128]{0,2,1:T(8,128)(2,1)}, u32[]{:S(2)}) copy-start(bf16[128,16,128]{0,2,1:T(8,128)(2,1)} %get-tuple-element.43) | copy-start | bytes 1572868
  (3 other events, 3.6 us)
Sparse Core Ops, SparseCore 0:
  10.2 76.9 all-gather.3
  364.5 49.3 all-gather.7
  416.8 72.9 all-gather.5
